TPU v7x, 32 devices: a whole 2x2x4 slice. The times are simulated.
32 devices in a mesh: dp: 2 (over y), gx: 4 (over x, core), gy: 4 (over z).
Axes of the slice: x: 2, y: 2, z: 4, core: 2. Of those that a mesh axis runs over, the one named last changes fastest.
Arguments:
- tokens: bfloat16 [2, 11664, 1152], P(None, ('dp', 'gy'), 'gx'), may hold values from -6 to 6
- cotangent: bfloat16 [2, 11664, 1152], P(None, ('dp', 'gy'), 'gx'), may hold values from -6 to 6
- ln1_gain: bfloat16 [1152], P('gx'), may hold values from 0.25 to 1.75
- ln1_bias: bfloat16 [1152], P('gx'), may hold values from -3 to 3
- qkv_weight: bfloat16 [1152, 3, 1152], P('gx', None, 'gy'), may hold values from -0.1875 to 0.1875
- qv_bias: bfloat16 [2, 1152], P(None, 'gy'), may hold values from -3 to 3
- out_weight: bfloat16 [1152, 1152], P('gy', 'gx'), may hold values from -1.5 to 1.5
- out_bias: bfloat16 [1152], P('gx'), may hold values from -3 to 3
- ln2_gain: bfloat16 [1152], P('gx'), may hold values from 0.25 to 1.75
- ln2_bias: bfloat16 [1152], P('gx'), may hold values from -3 to 3
- fc1_weight: bfloat16 [1152, 4304], P('gx', 'gy'), may hold values from -0.1875 to 0.1875
- fc1_bias: bfloat16 [4304], P('gy'), may hold values from -3 to 3
- fc2_weight: bfloat16 [4304, 1152], P('gy', 'gx'), may hold values from -0.09375 to 0.09375
- fc2_bias: bfloat16 [1152], P('gx'), may hold values from -3 to 3
Outputs:
- layer_out: bfloat16 [2, 11664, 1152], P(None, ('dp', 'gy'), 'gx')
- tokens_grad: bfloat16 [2, 11664, 1152], P(None, ('dp', 'gy'), 'gx')
- ln1_gain_grad: float32 [1152], P('gx')
- ln1_bias_grad: float32 [1152], P('gx')
- qkv_weight_grad: float32 [1152, 3, 1152], P('gx', None, 'gy')
- qv_bias_grad: float32 [2, 1152], P(None, 'gy')
- out_weight_grad: float32 [1152, 1152], P('gy', 'gx')
- out_bias_grad: float32 [1152], P('gx')
- ln2_gain_grad: float32 [1152], P('gx')
- ln2_bias_grad: float32 [1152], P('gx')
- fc1_weight_grad: float32 [1152, 4304], P('gx', 'gy')
- fc1_bias_grad: float32 [4304], P('gy')
- fc2_weight_grad: float32 [4304, 1152], P('gy', 'gx')
- fc2_bias_grad: float32 [1152], P('gx')
All inputs are finite; a program needn't handle non-finite values.
Results may differ from a plain program's by a relative error of at most 0.013.
The roundings to bfloat16 on the way count: a program that leaves them out, or rounds other values in their place, can miss the bound.
Values may be sent and summed in bfloat16 or wider, within the bound.
No kernel may reach another device: no remote copies, remote signals or barrier semaphores. Data moves between devices by JAX's collectives and lax.ppermute only.
A program may use at most 384 MiB of HBM per device.

v0:
```python
import jax
import jax.numpy as jnp
from jax import lax
from jax.sharding import PartitionSpec as P

HEAD_DIM = 72
SEQ = 729
MICRO = 2
epsilon = 1e-06


def contract_rows(left_side, right_side):
    return lax.dot_general(
        left_side, right_side, (((0,), (0,)), ((), ())), preferred_element_type=jnp.float32
    )


def contract_cols(left_side, right_side):
    return lax.dot_general(
        left_side, right_side, (((1,), (1,)), ((), ())), preferred_element_type=jnp.float32
    )


def apply_weight(rows, weight, backward):
    if backward:
        return contract_cols(rows, weight)
    return jnp.dot(rows, weight, preferred_element_type=jnp.float32)


def gelu_tanh(values):
    return jax.nn.gelu(values, approximate=True)


def row_pair_sums(first_terms, second_terms):
    return lax.psum((jnp.sum(first_terms, axis=1), jnp.sum(second_terms, axis=1)), "gx")


def norm_forward(values):
    row_sum, row_square = row_pair_sums(values, values * values)
    full_width = values.shape[1] * lax.axis_size("gx")
    center = row_sum / full_width
    spread = row_square / full_width - center * center
    inverse = lax.rsqrt(spread + epsilon)
    return ((values - center[:, None]) * inverse[:, None], inverse)


def norm_backward(grad_norm, normed, inverse, norm_gain):
    grad_hat = grad_norm * norm_gain
    row_sum, row_cross = row_pair_sums(grad_hat, grad_hat * normed)
    full_width = grad_norm.shape[1] * lax.axis_size("gx")
    return inverse[:, None] * (
        grad_hat - row_sum[:, None] / full_width - normed * (row_cross[:, None] / full_width)
    )


def spread(row_block, weight, backward):
    gathered = lax.all_gather(row_block, "gy", axis=0, tiled=True)
    full_rows = lax.all_to_all(gathered, "gx", split_axis=0, concat_axis=1, tiled=True)
    if backward:
        whole_weight = lax.all_gather(weight, "gx", axis=1, tiled=True)
    else:
        whole_weight = lax.all_gather(weight, "gx", axis=0, tiled=True)
    return (gathered, apply_weight(full_rows, whole_weight, backward))


def join(row_block, weight, backward):
    gathered = lax.all_gather(row_block, "gx", axis=0, tiled=True)
    full_rows = lax.all_to_all(gathered, "gy", split_axis=0, concat_axis=1, tiled=True)
    if backward:
        whole_weight = lax.all_gather(weight, "gy", axis=1, tiled=True)
    else:
        whole_weight = lax.all_gather(weight, "gy", axis=0, tiled=True)
    return (gathered, apply_weight(full_rows, whole_weight, backward))


def attend_image(packed):
    queries = packed[:, 0]
    key_rows = packed[:, 1]
    values = packed[:, 2]
    scaling = queries.shape[-1] ** (-0.5)
    scores = (
        jnp.einsum("qhd,khd->hqk", queries, key_rows, preferred_element_type=jnp.float32) * scaling
    )
    row_max = jnp.max(scores, axis=2, keepdims=True)
    exponent = jnp.exp(scores - row_max)
    row_total = jnp.sum(exponent, axis=2, keepdims=True)
    probability = (exponent / row_total).astype(jnp.bfloat16)
    mixture = jnp.einsum("hqk,khd->qhd", probability, values, preferred_element_type=jnp.float32)
    return (mixture.astype(jnp.bfloat16), (row_max + jnp.log(row_total))[:, :, 0])


def attend_backward(element):
    packed, log_total, grad_mixture = element
    queries = packed[:, 0]
    key_rows = packed[:, 1]
    values = packed[:, 2]
    scaling = queries.shape[-1] ** (-0.5)
    scores = (
        jnp.einsum("qhd,khd->hqk", queries, key_rows, preferred_element_type=jnp.float32) * scaling
    )
    probability = jnp.exp(scores - log_total[:, :, None])
    rounded = probability.astype(jnp.bfloat16)
    grad_values = jnp.einsum(
        "hqk,qhd->khd", rounded, grad_mixture, preferred_element_type=jnp.float32
    )
    grad_prob = jnp.einsum("qhd,khd->hqk", grad_mixture, values, preferred_element_type=jnp.float32)
    inner_sum = jnp.sum(probability * grad_prob, axis=2, keepdims=True)
    grad_scores = (probability * (grad_prob - inner_sum)).astype(jnp.bfloat16)
    grad_queries = (
        jnp.einsum("hqk,khd->qhd", grad_scores, key_rows, preferred_element_type=jnp.float32)
        * scaling
    )
    grad_keys = (
        jnp.einsum("hqk,qhd->khd", grad_scores, queries, preferred_element_type=jnp.float32)
        * scaling
    )
    return jnp.stack([grad_queries, grad_keys, grad_values], axis=1).astype(jnp.bfloat16)


def total_grads(mat_grads, row_grads):
    mat_summed = lax.psum(
        (
            mat_grads[0],
            mat_grads[1],
            mat_grads[2],
            mat_grads[3],
            mat_grads[4],
            mat_grads[5],
            mat_grads[6],
            mat_grads[7],
        ),
        "dp",
    )
    row_summed = lax.psum((row_grads[0], row_grads[1], row_grads[2], row_grads[3]), ("dp", "gy"))
    return (mat_summed, row_summed)


def on_device(
    tokens,
    cotangent,
    ln1_gain,
    ln1_bias,
    qkv_weight,
    qv_bias,
    out_weight,
    out_bias,
    ln2_gain,
    ln2_bias,
    fc1_weight,
    fc1_bias,
    fc2_weight,
    fc2_bias,
):
    width_local = qkv_weight.shape[0]
    head_cols = qkv_weight.shape[2]
    heads_here = head_cols // HEAD_DIM
    qkv_flat = qkv_weight.reshape(width_local, 3 * head_cols)
    bias_rows = (
        jnp.stack([qv_bias[0], jnp.zeros_like(qv_bias[0]), qv_bias[1]])
        .astype(jnp.float32)
        .reshape(1, 3 * head_cols)
    )
    gain_one = ln1_gain.astype(jnp.float32)
    shift_one = ln1_bias.astype(jnp.float32)
    gain_two = ln2_gain.astype(jnp.float32)
    shift_two = ln2_bias.astype(jnp.float32)
    bias_mix = out_bias.astype(jnp.float32)
    bias_first = fc1_bias.astype(jnp.float32)
    bias_second = fc2_bias.astype(jnp.float32)
    outputs = []
    grad_inputs = []
    mat_total = None
    row_total = None
    for batch_index in range(MICRO):
        current = tokens[batch_index].astype(jnp.float32)
        normed_one, inverse_one = norm_forward(current)
        ready_one = (normed_one * gain_one + shift_one).astype(jnp.bfloat16)
        gathered_one, projected = spread(ready_one, qkv_flat, False)
        projected = projected + bias_rows
        attn_rows = projected.shape[0]
        picture_count = attn_rows // SEQ
        packed = projected.astype(jnp.bfloat16).reshape(picture_count, SEQ, 3, heads_here, HEAD_DIM)
        mixture, log_total = lax.map(attend_image, packed)
        mixture = mixture.reshape(attn_rows, head_cols)
        gathered_mix, attn_out = join(mixture, out_weight, False)
        hidden = current + attn_out + bias_mix
        normed_two, inverse_two = norm_forward(hidden)
        ready_two = (normed_two * gain_two + shift_two).astype(jnp.bfloat16)
        gathered_two, first_out = spread(ready_two, fc1_weight, False)
        active, gelu_pull = jax.vjp(gelu_tanh, first_out + bias_first)
        gathered_act, second_out = join(active.astype(jnp.bfloat16), fc2_weight, False)
        outputs.append((hidden + second_out + bias_second).astype(jnp.bfloat16))
        grad_out = cotangent[batch_index]
        grad_out_all, grad_active = spread(grad_out, fc2_weight, True)
        grad_fc2 = contract_rows(gathered_act, grad_out_all)
        grad_fc2_bias = jnp.sum(grad_out_all, axis=0, dtype=jnp.float32)
        grad_first = gelu_pull(grad_active)[0].astype(jnp.bfloat16)
        grad_first_all, grad_ready_two = join(grad_first, fc1_weight, True)
        grad_fc1 = contract_rows(gathered_two, grad_first_all)
        grad_fc1_bias = jnp.sum(grad_first_all, axis=0, dtype=jnp.float32)
        grad_gain_two = jnp.sum(grad_ready_two * normed_two, axis=0)
        grad_shift_two = jnp.sum(grad_ready_two, axis=0)
        grad_hidden = grad_out.astype(jnp.float32) + norm_backward(
            grad_ready_two, normed_two, inverse_two, gain_two
        )
        grad_hidden_all, grad_mixture = spread(grad_hidden.astype(jnp.bfloat16), out_weight, True)
        grad_out_weight = contract_rows(gathered_mix, grad_hidden_all)
        grad_out_bias = jnp.sum(grad_hidden_all, axis=0, dtype=jnp.float32)
        grad_mix_low = grad_mixture.astype(jnp.bfloat16).reshape(
            picture_count, SEQ, heads_here, HEAD_DIM
        )
        grad_packed = lax.map(attend_backward, (packed, log_total, grad_mix_low))
        grad_packed = grad_packed.reshape(attn_rows, 3 * head_cols)
        grad_packed_all, grad_ready_one = join(grad_packed, qkv_flat, True)
        grad_qkv = contract_rows(gathered_one, grad_packed_all).reshape(width_local, 3, head_cols)
        col_sums = jnp.sum(grad_packed_all, axis=0, dtype=jnp.float32).reshape(3, head_cols)
        grad_qv = jnp.stack([col_sums[0], col_sums[2]])
        grad_gain_one = jnp.sum(grad_ready_one * normed_one, axis=0)
        grad_shift_one = jnp.sum(grad_ready_one, axis=0)
        grad_inputs.append(
            (grad_hidden + norm_backward(grad_ready_one, normed_one, inverse_one, gain_one)).astype(
                jnp.bfloat16
            )
        )
        mat_grads = (
            grad_qkv,
            grad_qv,
            grad_out_weight,
            grad_out_bias,
            grad_fc1,
            grad_fc1_bias,
            grad_fc2,
            grad_fc2_bias,
        )
        row_grads = (grad_gain_one, grad_shift_one, grad_gain_two, grad_shift_two)
        mat_grads, row_grads = total_grads(mat_grads, row_grads)
        if batch_index == 0:
            mat_total, row_total = (mat_grads, row_grads)
        else:
            mat_total = jax.tree.map(jnp.add, mat_total, mat_grads)
            row_total = jax.tree.map(jnp.add, row_total, row_grads)
    return (
        jnp.stack(outputs),
        jnp.stack(grad_inputs),
        row_total[0],
        row_total[1],
        mat_total[0],
        mat_total[1],
        mat_total[2],
        mat_total[3],
        row_total[2],
        row_total[3],
        mat_total[4],
        mat_total[5],
        mat_total[6],
        mat_total[7],
    )


def solution(mesh):
    return jax.shard_map(
        on_device,
        mesh=mesh,
        in_specs=(
            P(None, ("dp", "gy"), "gx"),
            P(None, ("dp", "gy"), "gx"),
            P("gx"),
            P("gx"),
            P("gx", None, "gy"),
            P(None, "gy"),
            P("gy", "gx"),
            P("gx"),
            P("gx"),
            P("gx"),
            P("gx", "gy"),
            P("gy"),
            P("gy", "gx"),
            P("gx"),
        ),
        out_specs=(
            P(None, ("dp", "gy"), "gx"),
            P(None, ("dp", "gy"), "gx"),
            P("gx"),
            P("gx"),
            P("gx", None, "gy"),
            P(None, "gy"),
            P("gy", "gx"),
            P("gx"),
            P("gx"),
            P("gx"),
            P("gx", "gy"),
            P("gy"),
            P("gy", "gx"),
            P("gx"),
        ),
        check_vma=False,
    )
```

profile of v0, /device:TPU:0, one launch (start us, length us, event | category | flops | bytes accessed | tf_op | source)
XLA Modules:
  0.0 3569.1 jit_solution(3430166739071463660)
XLA Ops:
  11.1 12.9 all-reduce.4
  28.3 68.2 %all-gather.52.cloned.1.call-done = bf16[4,1458,288]{1,2,0:T(8,128)(2,1)} async-done(((bf16[1,1458,288]{1,2,0:T(8,128)(2,1)}), bf16[4,1458,288]{1,2,0:T(8,128)(2,1)}) %all-gather.52.cloned.1.call-update) | async-done | bytes 3359248 | tf_op jit(solution)/shard_map/all_gather | solution.py:57
  101.5 65.8 %all-gather.62.cloned.1.call-done = bf16[4,1458,288]{1,2,0:T(8,128)(2,1)} async-done(((bf16[1,1458,288]{1,2,0:T(8,128)(2,1)}), bf16[4,1458,288]{1,2,0:T(8,128)(2,1)}) %all-gather.62.cloned.1.call-update) | async-done | bytes 3359248 | tf_op jit(solution)/shard_map/all_gather | solution.py:57
  172.0 29.6 all-gather.42.cloned.1.call-done
  285.7 26.1 all-gather.64.cloned.1.call-done
  311.8 53.7 %all-to-all-done.1 = bf16[4,1458,288]{1,2,0:T(8,128)(2,1)} async-done(((bf16[4,1458,288]{1,2,0:T(8,128)(2,1)}), bf16[4,1458,288]{1,2,0:T(8,128)(2,1)}, u32[]{:S(2)}, u32[]{:S(2)}) %all-to-all-start.1) | async-done | bytes 3359264 | tf_op jit(solution)/shard_map/all_to_all | solution.py:68
  379.5 187.2 %all_gather.83 = bf16[1152,288]{1,0:T(8,128)(2,1)S(1)} all-gather(bf16[288,288]{1,0:T(8,128)(2,1)} %param.28), channel_id=1, replica_groups=mesh['dp'=2,'gx'=4,'gy'=4] {'gy'}, dimensions={0}, use_global_device_ids=true | all-gather | bytes 829440 | tf_op jit(solution)/shard_map/all_gather | solution.py:72
  607.9 38.1 %reduce.2 = bf16[5832,288]{1,0:T(8,128)(2,1)} reduce(bf16[1,5832,288]{2,0,1:T(2,128)(2,1)} %all-gather.48.cloned.1.call-done, bf16[]{:T(256)} %constant.107), dimensions={0}, to_apply=%all-gather.reduce_sub_computation | reduce | bytes 6718466 | tf_op jit(solution)/shard_map/all_gather | solution.py:57
  663.8 54.7 %all-to-all-done.8 = bf16[4,1458,288]{1,2,0:T(8,128)(2,1)} async-done(((bf16[4,1458,288]{1,2,0:T(8,128)(2,1)}), bf16[4,1458,288]{1,2,0:T(8,128)(2,1)}, u32[]{:S(2)}, u32[]{:S(2)}) %all-to-all-start.8) | async-done | bytes 3359264 | tf_op jit(solution)/shard_map/all_to_all | solution.py:58
  733.6 26.0 all-gather.44.cloned.1.call-done
  759.6 19.1 all-to-all-done.2
  778.7 14.4 fusion.83
  793.1 126.9 %all-gather.50.cloned.1.call-done = bf16[1,5832,288]{2,0,1:T(2,128)(2,1)} async-done(((bf16[1,1458,288]{2,0,1:T(2,128)(2,1)}), bf16[1,5832,288]{2,0,1:T(2,128)(2,1)}) %all-gather.50.cloned.1.call-update) | async-done | bytes 3359248 | tf_op jit(solution)/shard_map/all_gather | solution.py:57
  920.0 38.1 %reduce.3 = bf16[5832,288]{1,0:T(8,128)(2,1)} reduce(bf16[1,5832,288]{2,0,1:T(2,128)(2,1)} %all-gather.50.cloned.1.call-done, bf16[]{:T(256)} %constant.107), dimensions={0}, to_apply=%all-gather.1.reduce_sub_computation | reduce | bytes 6718466 | tf_op jit(solution)/shard_map/all_gather | solution.py:57
  970.3 60.6 %all_to_all.304 = bf16[4,1458,288]{1,2,0:T(8,128)(2,1)} all-to-all(bf16[4,1458,288]{1,2,0:T(8,128)(2,1)} %copy.218), channel_id=1, replica_groups=mesh['dp'=2,'gx'=4,'gy'=4] {'gx'}, dimensions={0} | all-to-all | bytes 6718464 | tf_op jit(solution)/shard_map/all_to_all | solution.py:58
  1046.2 69.0 %all-to-all-done.6 = bf16[4,1458,288]{1,2,0:T(8,128)(2,1)} async-done(((bf16[4,1458,288]{1,2,0:T(8,128)(2,1)}), bf16[4,1458,288]{1,2,0:T(8,128)(2,1)}, u32[]{:S(2)}, u32[]{:S(2)}) %all-to-all-start.6) | async-done | bytes 3359264 | tf_op jit(solution)/shard_map/all_to_all | solution.py:58
  1115.2 14.1 fusion.82
  1136.2 76.6 %all-gather.80.cloned.1.call-done = bf16[4,1458,1076]{1,2,0:T(8,128)(2,1)} async-done(((bf16[1,1458,1076]{1,2,0:T(8,128)(2,1)}), bf16[4,1458,1076]{1,2,0:T(8,128)(2,1)}) %all-gather.80.cloned.1.call-update) | async-done | bytes 12550480 | tf_op jit(solution)/shard_map/all_gather | solution.py:67
  1212.8 210.8 %all-to-all-done.9 = bf16[4,1458,1076]{1,2,0:T(8,128)(2,1)} async-done(((bf16[4,1458,1076]{1,2,0:T(8,128)(2,1)}), bf16[4,1458,1076]{1,2,0:T(8,128)(2,1)}, u32[]{:S(2)}, u32[]{:S(2)}) %all-to-all-start.9) | async-done | bytes 12550496 | tf_op jit(solution)/shard_map/all_to_all | solution.py:68
  1430.9 138.4 %all-gather.72.cloned.1.call-done = bf16[4,1076,288]{1,2,0:T(8,128)(2,1)} async-done(((bf16[1,1076,288]{1,2,0:T(8,128)(2,1)}), bf16[4,1076,288]{1,2,0:T(8,128)(2,1)}) %all-gather.72.cloned.1.call-update) | async-done | bytes 2479120 | tf_op jit(solution)/shard_map/all_gather | solution.py:70
  1579.6 17.0 all_to_all.263
  1596.6 163.3 %all-to-all-done.13 = bf16[4,1458,1076]{1,2,0:T(8,128)(2,1)} async-done(((bf16[4,1458,1076]{1,2,0:T(8,128)(2,1)}), bf16[4,1458,1076]{1,2,0:T(8,128)(2,1)}, u32[]{:S(2)}, u32[]{:S(2)}) %all-to-all-start.13) | async-done | bytes 12550496 | tf_op jit(solution)/shard_map/all_to_all | solution.py:68
  1759.9 17.0 all_to_all.279
  1814.8 66.5 %all-gather.74.cloned.1.call-done = bf16[4,1458,288]{1,2,0:T(8,128)(2,1)} async-done(((bf16[1,1458,288]{1,2,0:T(8,128)(2,1)}), bf16[4,1458,288]{1,2,0:T(8,128)(2,1)}) %all-gather.74.cloned.1.call-update) | async-done | bytes 3359248 | tf_op jit(solution)/shard_map/all_gather | solution.py:57
  1885.1 114.2 %all-gather.58.cloned.1.call-done = bf16[4,1458,1076]{1,2,0:T(8,128)(2,1)} async-done(((bf16[1,1458,1076]{1,2,0:T(8,128)(2,1)}), bf16[4,1458,1076]{1,2,0:T(8,128)(2,1)}) %all-gather.58.cloned.1.call-update) | async-done | bytes 12550480 | tf_op jit(solution)/shard_map/all_gather | solution.py:67
  2025.3 59.5 %while.46 = (s32[]{:T(128)}, bf16[2,729,3,4,72]{1,4,3,2,0:T(8,128)(2,1)}, bf16[2,729,3,4,72]{1,4,3,2,0:T(8,128)(2,1)}, f32[2,4,729]{2,1,0:T(4,128)S(1)}, bf16[2,729,4,72]{1,3,2,0:T(8,128)(2,1)S(1)}, /*index=5*/s32[]{:T(128)}) while((s32[]{:T(128)}, bf16[2,729,3,4,72]{1,4,3,2,0:T(8,128)(2,1)}, bf16[2,729,3,4,72]{1,4,3,2,0:T(8,128)(2,1)}, ...), condition=%wide.region_30.31_spmd, body=%wide.region_28.30_spmd.sunk | while | flops 1560885248 | bytes 142425280 | solution.py:212
  2100.4 250.7 %all-to-all-done.3 = bf16[4,1458,1076]{1,2,0:T(8,128)(2,1)} async-done(((bf16[4,1458,1076]{1,2,0:T(8,128)(2,1)}), bf16[4,1458,1076]{1,2,0:T(8,128)(2,1)}, u32[]{:S(2)}, u32[]{:S(2)}) %all-to-all-start.3) | async-done | bytes 12550496 | tf_op jit(solution)/shard_map/all_to_all | solution.py:68
  2355.9 41.2 %all-to-all-done.14 = bf16[4,1458,288]{1,2,0:T(8,128)(2,1)} async-done(((bf16[4,1458,288]{1,2,0:T(8,128)(2,1)}), bf16[4,1458,288]{1,2,0:T(8,128)(2,1)}, u32[]{:S(2)}, u32[]{:S(2)}) %all-to-all-start.14) | async-done | bytes 3359264 | tf_op jit(solution)/shard_map/all_to_all | solution.py:58
  2411.6 59.4 %while.47 = (s32[]{:T(128)}, bf16[2,729,3,4,72]{1,4,3,2,0:T(8,128)(2,1)}, bf16[2,729,3,4,72]{1,4,3,2,0:T(8,128)(2,1)}, f32[2,4,729]{2,1,0:T(4,128)S(1)}, bf16[2,729,4,72]{1,3,2,0:T(8,128)(2,1)S(1)}, /*index=5*/s32[]{:T(128)}) while((s32[]{:T(128)}, bf16[2,729,3,4,72]{1,4,3,2,0:T(8,128)(2,1)}, bf16[2,729,3,4,72]{1,4,3,2,0:T(8,128)(2,1)}, ...), condition=%wide.region_41.42_spmd, body=%wide.region_39.41_spmd.sunk | while | flops 1560885248 | bytes 142425280 | solution.py:212
  2486.5 280.6 %all-to-all-done.7 = bf16[4,1458,1076]{1,2,0:T(8,128)(2,1)} async-done(((bf16[4,1458,1076]{1,2,0:T(8,128)(2,1)}), bf16[4,1458,1076]{1,2,0:T(8,128)(2,1)}, u32[]{:S(2)}, u32[]{:S(2)}) %all-to-all-start.7) | async-done | bytes 12550496 | tf_op jit(solution)/shard_map/all_to_all | solution.py:68
  2812.8 19.3 copy.238
  2832.1 20.9 copy.236
  2904.1 41.9 %copy.232 = bf16[4,1458,1076]{1,0,2:T(4,128)(2,1)} copy(bf16[4,1458,1076]{1,2,0:T(8,128)(2,1)} %all-gather.70.cloned.1.call-done) | data formatting | bytes 25100928 | tf_op jit(solution)/shard_map/all_gather | solution.py:67
  2946.0 25.3 reshape.342
  2971.3 41.8 %copy.234 = bf16[4,1458,1076]{1,0,2:T(4,128)(2,1)} copy(bf16[4,1458,1076]{1,2,0:T(8,128)(2,1)} %all-gather.80.cloned.1.call-done) | data formatting | bytes 25100928 | tf_op jit(solution)/shard_map/all_gather | solution.py:67
  3013.2 25.5 reshape.352
  3038.7 41.8 %copy.235 = bf16[4,1458,1076]{1,0,2:T(4,128)(2,1)} copy(bf16[4,1458,1076]{1,2,0:T(8,128)(2,1)} %all-gather.58.cloned.1.call-done) | data formatting | bytes 25100928 | tf_op jit(solution)/shard_map/all_gather | solution.py:67
  3080.5 25.3 reshape.330
  3105.8 41.8 %copy.237 = bf16[4,1458,1076]{1,0,2:T(4,128)(2,1)} copy(bf16[4,1458,1076]{1,2,0:T(8,128)(2,1)} %all-gather.68.cloned.1.call-done) | data formatting | bytes 25100928 | tf_op jit(solution)/shard_map/all_gather | solution.py:67
  3147.6 25.3 reshape.340
  3231.4 17.1 all_to_all.239
  3248.6 17.4 all_to_all.255
  3307.9 14.4 reshape.348
  3322.3 14.8 reshape.356
  3381.0 84.2 %all-reduce.9.cloned.1.call-done = (f32[288,3,288]{0,2,1:T(8,128)}, f32[288,288]{1,0:T(8,128)}, f32[288,1076]{1,0:T(8,128)}, f32[1076,288]{0,1:T(8,128)}) async-done(((f32[288,3,288]{0,2,1:T(8,128)}, f32[288,288]{1,0:T(8,128)}, f32[288,1076]{1,0:T(8,128)}, f32[1076,288]{0,1:T(8,128)}), (f32[288,3,288]{0,2,1:T(8,128)}, f32[288,288]{1,0:T(8,128)}, f32[288,1076]{1,0:T(8,128)}, ...) | async-done | bytes 3806224 | tf_op jit(solution)/shard_map/psum | solution.py:121
  3468.1 14.5 copy.213
  3482.6 14.5 copy.223
  3537.6 21.7 all-reduce
  (519 shorter events, 787.5 us)
Async XLA Ops:
  7.2 89.3 %all-gather.52.cloned.1.call-start = ((), (), s32[]{:S(2)}) async-start(), calls=%async_computation.21 | async-start | bytes 4423680 | tf_op jit(solution)/shard_map/all_gather | solution.py:57
  26.0 141.2 %all-gather.62.cloned.1.call-start = ((), (), s32[]{:S(2)}) async-start(), calls=%async_computation.26 | async-start | bytes 4423680 | tf_op jit(solution)/shard_map/all_gather | solution.py:57
  26.8 174.8 %all-gather.42.cloned.1.call-start = ((), (), s32[]{:S(2)}) async-start(), calls=%async_computation.16 | async-start | bytes 2580480 | tf_op jit(solution)/shard_map/all_gather | solution.py:62
  27.2 69.3 %copy-start.36 = (bf16[288,3,288]{0,2,1:T(8,128)(2,1)}, bf16[288,3,288]{0,2,1:T(8,128)(2,1)S(1)}, u32[]{:S(2)}) copy-start(bf16[288,3,288]{0,2,1:T(8,128)(2,1)S(1)} %copy.195) | copy-start | bytes 1492996
  28.3 73.0 %copy-start.96 = (bf16[2,288]{1,0:T(2,128)(2,1)S(1)}, bf16[2,288]{1,0:T(2,128)(2,1)}, u32[]{:S(2)}) copy-start(bf16[2,288]{1,0:T(2,128)(2,1)} %param.27) | copy-start | bytes 3460
  96.5 70.8 %all-to-all-start = ((bf16[4,1458,288]{1,2,0:T(8,128)(2,1)}), bf16[4,1458,288]{1,2,0:T(8,128)(2,1)}, u32[]{:S(2)}, u32[]{:S(2)}) async-start(bf16[4,1458,288]{1,2,0:T(8,128)(2,1)} %all-gather.52.cloned.1.call-done), calls=%async_computation | async-start | bytes 7077888 | tf_op jit(solution)/shard_map/all_to_all | solution.py:58
  167.3 71.7 %all-to-all-start.4 = ((bf16[4,1458,288]{1,2,0:T(8,128)(2,1)}), bf16[4,1458,288]{1,2,0:T(8,128)(2,1)}, u32[]{:S(2)}, u32[]{:S(2)}) async-start(bf16[4,1458,288]{1,2,0:T(8,128)(2,1)} %all-gather.62.cloned.1.call-done), calls=%async_computation.4 | async-start | bytes 7077888 | tf_op jit(solution)/shard_map/all_to_all | solution.py:58
  172.0 108.9 %all-gather.54.cloned.1.call-start = ((), (), s32[]{:S(2)}) async-start(), calls=%async_computation.22 | async-start | bytes 4423680 | tf_op jit(solution)/shard_map/all_gather | solution.py:67
  238.9 72.9 %all-gather.64.cloned.1.call-start = ((), (), s32[]{:S(2)}) async-start(), calls=%async_computation.27 | async-start | bytes 4423680 | tf_op jit(solution)/shard_map/all_gather | solution.py:67
  280.9 84.6 %all-to-all-start.1 = ((bf16[4,1458,288]{1,2,0:T(8,128)(2,1)}), bf16[4,1458,288]{1,2,0:T(8,128)(2,1)}, u32[]{:S(2)}, u32[]{:S(2)}) async-start(bf16[4,1458,288]{1,2,0:T(8,128)(2,1)} %all-gather.54.cloned.1.call-done), calls=%async_computation.1 | async-start | bytes 7077888 | tf_op jit(solution)/shard_map/all_to_all | solution.py:68
  285.7 84.6 %copy-start.10 = (bf16[2,1458,288]{1,2,0:T(8,128)(2,1)S(1)}, bf16[2,1458,288]{1,2,0:T(8,128)(2,1)}, u32[]{:S(2)}) copy-start(bf16[2,1458,288]{1,2,0:T(8,128)(2,1)} %param.23) | copy-start | bytes 5038852
  365.5 206.8 %all-to-all-start.5 = ((bf16[4,1458,288]{1,2,0:T(8,128)(2,1)}), bf16[4,1458,288]{1,2,0:T(8,128)(2,1)}, u32[]{:S(2)}, u32[]{:S(2)}) async-start(bf16[4,1458,288]{1,2,0:T(8,128)(2,1)} %all-gather.64.cloned.1.call-done), calls=%async_computation.5 | async-start | bytes 7077888 | tf_op jit(solution)/shard_map/all_to_all | solution.py:68
  370.2 237.6 %all-gather.48.cloned.1.call-start = ((), (), s32[]{:S(2)}) async-start(), calls=%async_computation.19 | async-start | bytes 11197440 | tf_op jit(solution)/shard_map/all_gather | solution.py:57
  371.6 195.9 %copy-start.8 = (bf16[2,1458,288]{1,2,0:T(8,128)(2,1)S(1)}, bf16[2,1458,288]{1,2,0:T(8,128)(2,1)}, u32[]{:S(2)}) copy-start(bf16[2,1458,288]{1,2,0:T(8,128)(2,1)} %param.22) | copy-start | bytes 5038852
  378.2 340.3 %all-gather.56.cloned.1.call-start = ((), (), s32[]{:S(2)}) async-start(), calls=%async_computation.23 | async-start | bytes 4423680 | tf_op jit(solution)/shard_map/all_gather | solution.py:57
  378.3 188.4 %copy-start.103 = (f32[288]{0:T(512)}, f32[288]{0:T(512)S(1)}, u32[]{:S(2)}) copy-start(f32[288]{0:T(512)S(1)} %convert_element_type.181) | copy-start | bytes 3460
  589.0 1219.0 %copy-start.60 = (f32[1458]{0:T(1024)}, f32[1458]{0:T(1024)S(1)}, u32[]{:S(2)}) copy-start(f32[1458]{0:T(1024)S(1)} %get-tuple-element.374) | copy-start | bytes 17500
  589.0 1219.0 %copy-start.62 = (f32[1458]{0:T(1024)}, f32[1458]{0:T(1024)S(1)}, u32[]{:S(2)}) copy-start(f32[1458]{0:T(1024)S(1)} %get-tuple-element.375) | copy-start | bytes 17500
  593.1 130.3 %all-gather.46.cloned.1.call-start = ((), (), s32[]{:S(2)}) async-start(), calls=%async_computation.18 | async-start | bytes 3317760 | tf_op jit(solution)/shard_map/all_gather | solution.py:60
  593.9 165.7 %all-gather.44.cloned.1.call-start = ((), (), s32[]{:S(2)}) async-start(), calls=%async_computation.17 | async-start | bytes 3317760 | tf_op jit(solution)/shard_map/all_gather | solution.py:62
  594.6 325.4 %all-gather.50.cloned.1.call-start = ((), (), s32[]{:S(2)}) async-start(), calls=%async_computation.20 | async-start | bytes 11197440 | tf_op jit(solution)/shard_map/all_gather | solution.py:57
  658.3 60.2 %all-to-all-start.8 = ((bf16[4,1458,288]{1,2,0:T(8,128)(2,1)}), bf16[4,1458,288]{1,2,0:T(8,128)(2,1)}, u32[]{:S(2)}, u32[]{:S(2)}) async-start(bf16[4,1458,288]{1,2,0:T(8,128)(2,1)} %copy.206), calls=%async_computation.8 | async-start | bytes 7077888 | tf_op jit(solution)/shard_map/all_to_all | solution.py:58
  663.0 367.9 %all-gather.66.cloned.1.call-start = ((), (), s32[]{:S(2)}) async-start(), calls=%async_computation.28 | async-start | bytes 4423680 | tf_op jit(solution)/shard_map/all_gather | solution.py:57
  663.8 59.5 %copy-start.97 = (bf16[1076]{0:T(1024)(128)(2,1)S(1)}, bf16[1076]{0:T(1024)(128)(2,1)}, u32[]{:S(2)}) copy-start(bf16[1076]{0:T(1024)(128)(2,1)} %param.33) | copy-start | bytes 6460
  718.5 60.2 %all-to-all-start.2 = ((bf16[4,1458,288]{1,2,0:T(8,128)(2,1)}), bf16[4,1458,288]{1,2,0:T(8,128)(2,1)}, u32[]{:S(2)}, u32[]{:S(2)}) async-start(bf16[4,1458,288]{1,2,0:T(8,128)(2,1)} %all-gather.56.cloned.1.call-done), calls=%async_computation.2 | async-start | bytes 7077888 | tf_op jit(solution)/shard_map/all_to_all | solution.py:58
  723.2 406.1 %all-gather.70.cloned.1.call-start = ((), (), s32[]{:S(2)}) async-start(), calls=%async_computation.30 | async-start | bytes 16588800 | tf_op jit(solution)/shard_map/all_gather | solution.py:67
  1030.9 84.2 %all-to-all-start.6 = ((bf16[4,1458,288]{1,2,0:T(8,128)(2,1)}), bf16[4,1458,288]{1,2,0:T(8,128)(2,1)}, u32[]{:S(2)}, u32[]{:S(2)}) async-start(bf16[4,1458,288]{1,2,0:T(8,128)(2,1)} %all-gather.66.cloned.1.call-done), calls=%async_computation.6 | async-start | bytes 7077888 | tf_op jit(solution)/shard_map/all_to_all | solution.py:58
  1035.7 177.1 %all-gather.80.cloned.1.call-start = ((), (), s32[]{:S(2)}) async-start(), calls=%async_computation.35 | async-start | bytes 16588800 | tf_op jit(solution)/shard_map/all_gather | solution.py:67
  1129.4 294.2 %all-to-all-start.9 = ((bf16[4,1458,1076]{1,2,0:T(8,128)(2,1)}), bf16[4,1458,1076]{1,2,0:T(8,128)(2,1)}, u32[]{:S(2)}, u32[]{:S(2)}) async-start(bf16[4,1458,1076]{1,2,0:T(8,128)(2,1)} %all-gather.70.cloned.1.call-done), calls=%async_computation.9 | async-start | bytes 26542080 | tf_op jit(solution)/shard_map/all_to_all | solution.py:68
  1423.6 336.3 %all-to-all-start.13 = ((bf16[4,1458,1076]{1,2,0:T(8,128)(2,1)}), bf16[4,1458,1076]{1,2,0:T(8,128)(2,1)}, u32[]{:S(2)}, u32[]{:S(2)}) async-start(bf16[4,1458,1076]{1,2,0:T(8,128)(2,1)} %all-gather.80.cloned.1.call-done), calls=%async_computation.13 | async-start | bytes 26542080 | tf_op jit(solution)/shard_map/all_to_all | solution.py:68
  1430.1 139.2 %all-gather.72.cloned.1.call-start = ((), (), s32[]{:S(2)}) async-start(), calls=%async_computation.31 | async-start | bytes 3317760 | tf_op jit(solution)/shard_map/all_gather | solution.py:70
  1430.6 450.7 %all-gather.74.cloned.1.call-start = ((), (), s32[]{:S(2)}) async-start(), calls=%async_computation.32 | async-start | bytes 4423680 | tf_op jit(solution)/shard_map/all_gather | solution.py:57
  1813.0 186.2 %all-gather.58.cloned.1.call-start = ((), (), s32[]{:S(2)}) async-start(), calls=%async_computation.24 | async-start | bytes 16588800 | tf_op jit(solution)/shard_map/all_gather | solution.py:67
  1813.6 537.5 %all-gather.82.cloned.1.call-start = ((), (), s32[]{:S(2)}) async-start(), calls=%async_computation.36 | async-start | bytes 4423680 | tf_op jit(solution)/shard_map/all_gather | solution.py:57
  1814.2 541.7 %all-gather.68.cloned.1.call-start = ((), (), s32[]{:S(2)}) async-start(), calls=%async_computation.29 | async-start | bytes 16588800 | tf_op jit(solution)/shard_map/all_gather | solution.py:67
  1881.3 118.0 %all-to-all-start.10 = ((bf16[4,1458,288]{1,2,0:T(8,128)(2,1)}), bf16[4,1458,288]{1,2,0:T(8,128)(2,1)S(1)}, u32[]{:S(2)}, u32[]{:S(2)}) async-start(bf16[4,1458,288]{1,2,0:T(8,128)(2,1)} %all-gather.74.cloned.1.call-done), calls=%async_computation.10 | async-start | bytes 7077888 | tf_op jit(solution)/shard_map/all_to_all | solution.py:58
  1999.3 351.8 %all-to-all-start.3 = ((bf16[4,1458,1076]{1,2,0:T(8,128)(2,1)}), bf16[4,1458,1076]{1,2,0:T(8,128)(2,1)}, u32[]{:S(2)}, u32[]{:S(2)}) async-start(bf16[4,1458,1076]{1,2,0:T(8,128)(2,1)} %all-gather.58.cloned.1.call-done), calls=%async_computation.3 | async-start | bytes 26542080 | tf_op jit(solution)/shard_map/all_to_all | solution.py:68
  2005.8 761.4 %all-gather.76.cloned.1.call-start = ((), (), s32[]{:S(2)}) async-start(), calls=%async_computation.33 | async-start | bytes 13117440 | tf_op jit(solution)/shard_map/all_gather | solution.py:67
  2351.1 46.0 %all-to-all-start.14 = ((bf16[4,1458,288]{1,2,0:T(8,128)(2,1)}), bf16[4,1458,288]{1,2,0:T(8,128)(2,1)}, u32[]{:S(2)}, u32[]{:S(2)}) async-start(bf16[4,1458,288]{1,2,0:T(8,128)(2,1)} %all-gather.82.cloned.1.call-done), calls=%async_computation.14 | async-start | bytes 7077888 | tf_op jit(solution)/shard_map/all_to_all | solution.py:58
  2355.9 49.8 %copy-start.50 = (bf16[288,1152]{0,1:T(8,128)(2,1)S(1)}, bf16[288,1152]{0,1:T(8,128)(2,1)}, u32[]{:S(2)}) copy-start(bf16[288,1152]{0,1:T(8,128)(2,1)} %copy-done.49) | copy-start | bytes 1990660
  2397.1 370.1 %all-to-all-start.7 = ((bf16[4,1458,1076]{1,2,0:T(8,128)(2,1)}), bf16[4,1458,1076]{1,2,0:T(8,128)(2,1)}, u32[]{:S(2)}, u32[]{:S(2)}) async-start(bf16[4,1458,1076]{1,2,0:T(8,128)(2,1)} %all-gather.68.cloned.1.call-done), calls=%async_computation.7 | async-start | bytes 26542080 | tf_op jit(solution)/shard_map/all_to_all | solution.py:68
  2403.5 370.5 %all-gather.78.cloned.1.call-start = ((), (), s32[]{:S(2)}) async-start(), calls=%async_computation.34 | async-start | bytes 2580480 | tf_op jit(solution)/shard_map/all_gather | solution.py:70
  2404.7 374.7 %all-gather.60.cloned.1.call-start = ((), (), s32[]{:S(2)}) async-start(), calls=%async_computation.25 | async-start | bytes 3317760 | tf_op jit(solution)/shard_map/all_gather | solution.py:72
  2405.4 767.5 %all-gather.84.cloned.1.call-start = ((), (), s32[]{:S(2)}) async-start(), calls=%async_computation.37 | async-start | bytes 13117440 | tf_op jit(solution)/shard_map/all_gather | solution.py:67
  2486.5 286.9 %copy-start.109 = (bf16[288]{0:T(512)(128)(2,1)S(1)}, bf16[288]{0:T(512)(128)(2,1)}, u32[]{:S(2)}) copy-start(bf16[288]{0:T(512)(128)(2,1)} %param.35) | copy-start | bytes 1732
  2767.2 405.8 %all-to-all-start.11 = ((bf16[4,1458,864]{2,1,0:T(8,128)(2,1)}), bf16[4,1458,864]{2,1,0:T(8,128)(2,1)}, u32[]{:S(2)}, u32[]{:S(2)}) async-start(bf16[4,1458,864]{2,1,0:T(8,128)(2,1)} %all-gather.76.cloned.1.call-done), calls=%async_computation.11 | async-start | bytes 20987904 | tf_op jit(solution)/shard_map/all_to_all | solution.py:68
  3172.9 309.7 %all-to-all-start.15 = ((bf16[4,1458,864]{2,1,0:T(8,128)(2,1)}), bf16[4,1458,864]{2,1,0:T(8,128)(2,1)}, u32[]{:S(2)}, u32[]{:S(2)}) async-start(bf16[4,1458,864]{2,1,0:T(8,128)(2,1)} %all-gather.84.cloned.1.call-done), calls=%async_computation.15 | async-start | bytes 20987904 | tf_op jit(solution)/shard_map/all_to_all | solution.py:68
  3179.0 286.2 %all-reduce.9.cloned.1.call-start = ((), (), s32[]{:S(2)}) async-start(), calls=%async_computation.38 | async-start | bytes 8847360 | tf_op jit(solution)/shard_map/psum | solution.py:121
  (111 other events, 916.3 us)
Sparse Core Ops, SparseCore 0:
  26.2 70.3 all-gather.51
  98.6 68.5 all-gather.61
  169.4 32.1 all-gather.41
  239.0 30.7 all-gather.53
  281.0 30.7 all-gather.63
  378.3 229.4 all-gather.47
  610.0 68.0 all-gather.55
  679.6 38.6 all-gather.45
  719.9 39.6 all-gather.43
  761.0 158.9 all-gather.49
  922.1 68.1 all-gather.65
  991.8 136.1 all-gather.69
  1129.5 83.2 all-gather.79
  1432.2 137.0 all-gather.71
  1813.2 68.1 all-gather.73
  1882.7 116.4 all-gather.57
  2001.3 166.1 all-gather.81
  2168.9 83.2 all-gather.67
  2253.8 70.2 all-gather.75
  2406.2 122.8 all-gather.77
  2530.7 91.3 all-gather.59
  2623.7 163.8 all-gather.83
  3350.5 114.6 all-reduce.8
where the time goes:
time: 3590 us; the launch traced here: 3570 us
  waiting for transfers between devices  1980 us (55%)
  local copies, waits for them, and re-layouts  705 us (20%)
  blocking collectives  336 us (9%)
  matrix products  263 us (7%)
  other arithmetic  187 us (5%)
  starting transfers between devices  82.3 us (2%)
    all_to_all x8, waiting for transfers between devices, join(): lax.all_to_all(gathered, 'gy', split_axis=0, concat_axis=1, tiled=True)  959 us
    all_gather x8, waiting for transfers between devices, spread(): gathered = lax.all_gather(row_block, 'gy', axis=0, tiled=True)  336 us
    unnamed x240, local copies, waits for them, and re-layouts  258 us
    all_gather x8, waiting for transfers between devices, join(): gathered = lax.all_gather(row_block, 'gx', axis=0, tiled=True)  217 us
    all_gather x1, blocking collectives, join(): whole_weight = lax.all_gather(weight, 'gy', axis=0, tiled=True)  187 us
    all_to_all x7, waiting for transfers between devices, spread(): lax.all_to_all(gathered, 'gx', split_axis=0, concat_axis=1, tiled=True)  184 us
    all_gather x6, local copies, waits for them, and re-layouts, join(): gathered = lax.all_gather(row_block, 'gx', axis=0, tiled=True)  176 us
    all_gather x2, waiting for transfers between devices, join(): whole_weight = lax.all_gather(weight, 'gy', axis=1, tiled=True)  138 us
  transfers between devices with their start and end apart: 38, of which 21 were waited for; matrix products, arithmetic and copies ran while one was open for 28% of the time, Pallas kernels for 0%

commit v1 on v0

--- a/solution.py
+++ b/solution.py
@@ -7,6 +7,19 @@
 SEQ = 729
 MICRO = 2
 epsilon = 1e-06
+
+
+def arrange_stops_all_by_axis(mine_x, d_out, mine):
+    z2, top = (mine_x.shape[:d_out], mine_x.shape[d_out + 1 :])
+    latest = jnp.moveaxis(mine_x.reshape(*z2, mine, -1, *top), d_out, 0)
+    return latest
+
+
+def measure_ladders(block_in, row_dim):
+    k_now = list(block_in.shape[1:])
+    k_now[row_dim] *= block_in.shape[0]
+    view_out = jnp.moveaxis(block_in, 0, row_dim).reshape(k_now)
+    return view_out
 
 
 def contract_rows(left_side, right_side):
@@ -55,7 +68,21 @@
 
 def spread(row_block, weight, backward):
     gathered = lax.all_gather(row_block, "gy", axis=0, tiled=True)
-    full_rows = lax.all_to_all(gathered, "gx", split_axis=0, concat_axis=1, tiled=True)
+
+    def open_the_slices(payload, mesh_dim, u_in, chunk):
+        shaped, q_next = (lax.axis_size(mesh_dim), lax.axis_index(mesh_dim))
+        tall = arrange_stops_all_by_axis(payload, u_in, shaped)
+        blocks_here = [tall[q_next]]
+        for ix in [*range(1, shaped)]:
+            low = tall[q_next ^ ix]
+            blocks_here.append(
+                lax.ppermute(low, axis_name=mesh_dim, perm=[(b, b ^ ix) for b in range(shaped)])
+            )
+        tall = jnp.stack(blocks_here)[q_next ^ jnp.arange(shaped)]
+        d_next = measure_ladders(tall, chunk)
+        return d_next
+
+    full_rows = open_the_slices(gathered, "gx", 0, 1)
     if backward:
         whole_weight = lax.all_gather(weight, "gx", axis=1, tiled=True)
     else:

time: 3590 us -> 3350 us (0.933)
  waiting for transfers between devices: 1980 us -> 1790 us
  other arithmetic: 187 us -> 124 us
  local copies, waits for them, and re-layouts: 705 us -> 760 us
    ppermute x0 -> x24, waiting for transfers between devices: none -> 270 us  [open_the_slices(): lax.ppermute(low, axis_name=mesh_dim, perm=[(b, b ^ ix) for b in range(sh...]
    all_to_all x8, waiting for transfers between devices: 959 us -> 754 us  [join(): lax.all_to_all(gathered, 'gy', split_axis=0, concat_axis=1, tiled=True)]
    all_to_all x7 -> x0, waiting for transfers between devices: 184 us -> none  [spread(): lax.all_to_all(gathered, 'gx', split_axis=0, concat_axis=1, tiled=True)]
    all_gather x8, waiting for transfers between devices: 217 us -> 117 us  [join(): gathered = lax.all_gather(row_block, 'gx', axis=0, tiled=True)]
    all_gather x2 -> x0, other arithmetic: 76.3 us -> none  [spread(): gathered = lax.all_gather(row_block, 'gy', axis=0, tiled=True)]
    all_gather x1, blocking collectives: 9.36 us -> 82.9 us  [spread(): whole_weight = lax.all_gather(weight, 'gx', axis=1, tiled=True)]
    all_gather x8, waiting for transfers between devices: 336 us -> 403 us  [spread(): gathered = lax.all_gather(row_block, 'gy', axis=0, tiled=True)]
    all_to_all x1 -> x0, blocking collectives: 60.6 us -> none  [spread(): lax.all_to_all(gathered, 'gx', split_axis=0, concat_axis=1, tiled=True)]
  transfers between devices with their start and end apart: 38 -> 55, of which waited for: 21 -> 26; matrix products, arithmetic and copies ran while one was open for 28% -> 30% of each run, Pallas kernels for 0% -> 0%
where the time goes in v1:
time: 3350 us; the launch traced here: 3340 us
  waiting for transfers between devices  1790 us (53%)
  local copies, waits for them, and re-layouts  760 us (23%)
  blocking collectives  320 us (10%)
  matrix products  260 us (8%)
  other arithmetic  124 us (4%)
  starting transfers between devices  67.1 us (2%)
    all_to_all x8, waiting for transfers between devices, join(): lax.all_to_all(gathered, 'gy', split_axis=0, concat_axis=1, tiled=True)  754 us
    all_gather x8, waiting for transfers between devices, spread(): gathered = lax.all_gather(row_block, 'gy', axis=0, tiled=True)  403 us
    ppermute x24, waiting for transfers between devices, open_the_slices(): lax.ppermute(low, axis_name=mesh_dim, perm=[(b, b ^ ix) for b in range(sh...  270 us
    unnamed x270, local copies, waits for them, and re-layouts  259 us
    all_gather x6, local copies, waits for them, and re-layouts, join(): gathered = lax.all_gather(row_block, 'gx', axis=0, tiled=True)  180 us
    all_gather x1, blocking collectives, join(): whole_weight = lax.all_gather(weight, 'gy', axis=0, tiled=True)  159 us
    all_gather x2, waiting for transfers between devices, join(): whole_weight = lax.all_gather(weight, 'gy', axis=1, tiled=True)  138 us
    all_gather x8, waiting for transfers between devices, join(): gathered = lax.all_gather(row_block, 'gx', axis=0, tiled=True)  117 us
  transfers between devices with their start and end apart: 55, of which 26 were waited for; matrix products, arithmetic and copies ran while one was open for 30% of the time, Pallas kernels for 0%

profile of v1, /device:TPU:0, one launch (start us, length us, event | category | flops | bytes accessed | tf_op | source)
XLA Modules:
  0.0 3340.2 jit_solution(10832000872825968341)
XLA Ops:
  28.7 67.8 %all-gather.52.cloned.1.call-done = bf16[4,1458,288]{1,2,0:T(8,128)(2,1)} async-done(((bf16[1,1458,288]{1,2,0:T(8,128)(2,1)}), bf16[4,1458,288]{1,2,0:T(8,128)(2,1)}) %all-gather.52.cloned.1.call-update) | async-done | bytes 3359248 | tf_op jit(solution)/shard_map/all_gather | solution.py:70
  102.1 65.2 %all-gather.62.cloned.1.call-done = bf16[4,1458,288]{1,2,0:T(8,128)(2,1)} async-done(((bf16[1,1458,288]{1,2,0:T(8,128)(2,1)}), bf16[4,1458,288]{1,2,0:T(8,128)(2,1)}) %all-gather.62.cloned.1.call-update) | async-done | bytes 3359248 | tf_op jit(solution)/shard_map/all_gather | solution.py:70
  179.0 22.0 all-gather.42.cloned.1.call-done
  295.5 20.3 all-gather.64.cloned.1.call-done
  315.9 114.8 %all-to-all-done = bf16[4,1458,288]{1,2,0:T(8,128)(2,1)} async-done(((bf16[4,1458,288]{1,2,0:T(8,128)(2,1)}), bf16[4,1458,288]{1,2,0:T(8,128)(2,1)}, u32[]{:S(2)}, u32[]{:S(2)}) %all-to-all-start) | async-done | bytes 3359264 | tf_op jit(solution)/shard_map/all_to_all | solution.py:95
  441.3 159.0 %all_gather.83 = bf16[1152,288]{1,0:T(8,128)(2,1)S(1)} all-gather(bf16[288,288]{1,0:T(8,128)(2,1)S(1)} %copy-done.60), channel_id=1, replica_groups=mesh['dp'=2,'gx'=4,'gy'=4] {'gy'}, dimensions={0}, use_global_device_ids=true | all-gather | bytes 829440 | tf_op jit(solution)/shard_map/all_gather | solution.py:99
  626.6 19.3 copy.156
  652.8 109.9 %all-gather.50.cloned.1.call-done = bf16[1,5832,288]{2,0,1:T(2,128)(2,1)} async-done(((bf16[1,1458,288]{2,0,1:T(2,128)(2,1)}), bf16[1,5832,288]{2,0,1:T(2,128)(2,1)}) %all-gather.50.cloned.1.call-update) | async-done | bytes 3359248 | tf_op jit(solution)/shard_map/all_gather | solution.py:70
  762.7 19.3 copy.168
  790.3 19.1 constant_dynamic-slice_fusion.4
  812.6 19.7 collective-permute-done.13
  832.3 26.5 collective-permute-done.14
  877.2 25.7 collective-permute-done.4
  902.9 18.5 collective-permute-done.5
  945.4 20.4 collective-permute-done.19
  965.7 17.4 collective-permute-done.20
  998.5 32.3 collective-permute-done.10
  1030.8 37.3 %collective-permute-done.11 = bf16[1458,288]{0,1:T(8,128)(2,1)S(1)} collective-permute-done((bf16[1458,288]{0,1:T(8,128)(2,1)S(1)}, bf16[1458,288]{0,1:T(8,128)(2,1)S(1)}, u32[]{:S(2)}, u32[]{:S(2)}) %collective-permute-start.11) | collective-permute-done | bytes 839840 | tf_op jit(solution)/shard_map/ppermute | solution.py:79
  1085.4 18.0 all-gather.70.cloned.1.call-done
  1109.9 78.4 %all-gather.80.cloned.1.call-done = bf16[4,1458,1076]{1,2,0:T(8,128)(2,1)} async-done(((bf16[1,1458,1076]{1,2,0:T(8,128)(2,1)}), bf16[4,1458,1076]{1,2,0:T(8,128)(2,1)}) %all-gather.80.cloned.1.call-update) | async-done | bytes 12550480 | tf_op jit(solution)/shard_map/all_gather | solution.py:94
  1188.3 210.0 %all-to-all-done.4 = bf16[4,1458,1076]{1,2,0:T(8,128)(2,1)} async-done(((bf16[4,1458,1076]{1,2,0:T(8,128)(2,1)}), bf16[4,1458,1076]{1,2,0:T(8,128)(2,1)}, u32[]{:S(2)}, u32[]{:S(2)}) %all-to-all-start.4) | async-done | bytes 12550496 | tf_op jit(solution)/shard_map/all_to_all | solution.py:95
  1405.9 138.4 %all-gather.72.cloned.1.call-done = bf16[4,1076,288]{1,2,0:T(8,128)(2,1)} async-done(((bf16[1,1076,288]{1,2,0:T(8,128)(2,1)}), bf16[4,1076,288]{1,2,0:T(8,128)(2,1)}) %all-gather.72.cloned.1.call-update) | async-done | bytes 2479120 | tf_op jit(solution)/shard_map/all_gather | solution.py:97
  1550.8 18.2 all_to_all.131
  1569.0 165.9 %all-to-all-done.6 = bf16[4,1458,1076]{1,2,0:T(8,128)(2,1)} async-done(((bf16[4,1458,1076]{1,2,0:T(8,128)(2,1)}), bf16[4,1458,1076]{1,2,0:T(8,128)(2,1)}, u32[]{:S(2)}, u32[]{:S(2)}) %all-to-all-start.6) | async-done | bytes 12550496 | tf_op jit(solution)/shard_map/all_to_all | solution.py:95
  1735.0 17.1 all_to_all.139
  1796.6 160.2 %all-gather.74.cloned.1.call-done = bf16[4,1458,288]{1,2,0:T(8,128)(2,1)} async-done(((bf16[1,1458,288]{1,2,0:T(8,128)(2,1)}), bf16[4,1458,288]{1,2,0:T(8,128)(2,1)}) %all-gather.74.cloned.1.call-update) | async-done | bytes 3359248 | tf_op jit(solution)/shard_map/all_gather | solution.py:70
  1962.6 82.9 %all_gather.97 = bf16[288,1152]{0,1:T(8,128)(2,1)} all-gather(bf16[288,288]{0,1:T(8,128)(2,1)S(1)} %copy.159), channel_id=1, replica_groups=mesh['dp'=2,'gx'=4,'gy'=4] {'gx'}, dimensions={1}, use_global_device_ids=true | all-gather | bytes 829440 | tf_op jit(solution)/shard_map/all_gather | solution.py:87
  2058.4 59.7 %while.46 = (s32[]{:T(128)}, bf16[2,729,3,4,72]{1,4,3,2,0:T(8,128)(2,1)}, bf16[2,729,3,4,72]{1,4,3,2,0:T(8,128)(2,1)}, f32[2,4,729]{2,1,0:T(4,128)S(1)}, bf16[2,729,4,72]{1,3,2,0:T(8,128)(2,1)S(1)}, /*index=5*/s32[]{:T(128)}) while((s32[]{:T(128)}, bf16[2,729,3,4,72]{1,4,3,2,0:T(8,128)(2,1)}, bf16[2,729,3,4,72]{1,4,3,2,0:T(8,128)(2,1)}, ...), condition=%wide.region_30.31_spmd, body=%wide.region_28.30_spmd.sunk | while | flops 1560885248 | bytes 142425280 | solution.py:239
  2133.6 65.1 %all-to-all-done.1 = bf16[4,1458,1076]{1,2,0:T(8,128)(2,1)} async-done(((bf16[4,1458,1076]{1,2,0:T(8,128)(2,1)}), bf16[4,1458,1076]{1,2,0:T(8,128)(2,1)}, u32[]{:S(2)}, u32[]{:S(2)}) %all-to-all-start.1) | async-done | bytes 12550496 | tf_op jit(solution)/shard_map/all_to_all | solution.py:95
  2212.8 39.0 %collective-permute-done.22 = bf16[1458,288]{0,1:T(8,128)(2,1)S(1)} collective-permute-done((bf16[1458,288]{0,1:T(8,128)(2,1)}, bf16[1458,288]{0,1:T(8,128)(2,1)S(1)}, u32[]{:S(2)}, u32[]{:S(2)}) %collective-permute-start.22) | collective-permute-done | bytes 839840 | tf_op jit(solution)/shard_map/ppermute | solution.py:79
  2251.8 32.7 collective-permute-done.23
  2296.8 59.5 %while.47 = (s32[]{:T(128)}, bf16[2,729,3,4,72]{1,4,3,2,0:T(8,128)(2,1)}, bf16[2,729,3,4,72]{1,4,3,2,0:T(8,128)(2,1)}, f32[2,4,729]{2,1,0:T(4,128)S(1)}, bf16[2,729,4,72]{1,3,2,0:T(8,128)(2,1)S(1)}, /*index=5*/s32[]{:T(128)}) while((s32[]{:T(128)}, bf16[2,729,3,4,72]{1,4,3,2,0:T(8,128)(2,1)}, bf16[2,729,3,4,72]{1,4,3,2,0:T(8,128)(2,1)}, ...), condition=%wide.region_41.42_spmd, body=%wide.region_39.41_spmd.sunk | while | flops 1560885248 | bytes 142425280 | solution.py:239
  2371.8 197.9 %all-to-all-done.3 = bf16[4,1458,1076]{1,2,0:T(8,128)(2,1)} async-done(((bf16[4,1458,1076]{1,2,0:T(8,128)(2,1)}), bf16[4,1458,1076]{1,2,0:T(8,128)(2,1)}, u32[]{:S(2)}, u32[]{:S(2)}) %all-to-all-start.3) | async-done | bytes 12550496 | tf_op jit(solution)/shard_map/all_to_all | solution.py:95
  2673.1 41.8 %copy.183 = bf16[4,1458,1076]{1,0,2:T(4,128)(2,1)} copy(bf16[4,1458,1076]{1,2,0:T(8,128)(2,1)} %all-gather.70.cloned.1.call-done) | data formatting | bytes 25100928 | tf_op jit(solution)/shard_map/all_gather | solution.py:94
  2715.0 25.3 reshape.462
  2740.3 41.8 %copy.185 = bf16[4,1458,1076]{1,0,2:T(4,128)(2,1)} copy(bf16[4,1458,1076]{1,2,0:T(8,128)(2,1)} %all-gather.80.cloned.1.call-done) | data formatting | bytes 25100928 | tf_op jit(solution)/shard_map/all_gather | solution.py:94
  2782.1 25.7 reshape.472
  2807.8 41.8 %copy.186 = bf16[4,1458,1076]{1,0,2:T(4,128)(2,1)} copy(bf16[4,1458,1076]{1,2,0:T(8,128)(2,1)} %all-gather.58.cloned.1.call-done) | data formatting | bytes 25100928 | tf_op jit(solution)/shard_map/all_gather | solution.py:94
  2849.7 25.3 reshape.450
  2875.0 41.8 %copy.188 = bf16[4,1458,1076]{1,0,2:T(4,128)(2,1)} copy(bf16[4,1458,1076]{1,2,0:T(8,128)(2,1)} %all-gather.68.cloned.1.call-done) | data formatting | bytes 25100928 | tf_op jit(solution)/shard_map/all_gather | solution.py:94
  2916.9 25.3 reshape.460
  3002.3 17.1 all_to_all.119
  3019.4 17.6 all_to_all.127
  3078.7 14.5 reshape.468
  3093.2 15.1 reshape.476
  3152.2 84.2 %all-reduce.9.cloned.1.call-done = (f32[288,3,288]{0,2,1:T(8,128)}, f32[288,288]{1,0:T(8,128)}, f32[288,1076]{1,0:T(8,128)}, f32[1076,288]{0,1:T(8,128)}) async-done(((f32[288,3,288]{0,2,1:T(8,128)}, f32[288,288]{1,0:T(8,128)}, f32[288,1076]{1,0:T(8,128)}, f32[1076,288]{0,1:T(8,128)}), (f32[288,3,288]{0,2,1:T(8,128)}, f32[288,288]{1,0:T(8,128)}, f32[288,1076]{1,0:T(8,128)}, ...) | async-done | bytes 3806224 | tf_op jit(solution)/shard_map/psum | solution.py:148
  3239.3 14.6 copy.164
  3308.9 21.6 all-reduce
  (605 shorter events, 854.9 us)
Async XLA Ops:
  7.2 89.3 %all-gather.52.cloned.1.call-start = ((), (), s32[]{:S(2)}) async-start(), calls=%async_computation.13 | async-start | bytes 4423680 | tf_op jit(solution)/shard_map/all_gather | solution.py:70
  26.0 141.2 %all-gather.62.cloned.1.call-start = ((), (), s32[]{:S(2)}) async-start(), calls=%async_computation.18 | async-start | bytes 4423680 | tf_op jit(solution)/shard_map/all_gather | solution.py:70
  26.8 174.2 %all-gather.42.cloned.1.call-start = ((), (), s32[]{:S(2)}) async-start(), calls=%async_computation.8 | async-start | bytes 2580480 | tf_op jit(solution)/shard_map/all_gather | solution.py:89
  28.3 256.2 %all-gather.54.cloned.1.call-start = ((), (), s32[]{:S(2)}) async-start(), calls=%async_computation.14 | async-start | bytes 4423680 | tf_op jit(solution)/shard_map/all_gather | solution.py:94
  100.0 72.6 %collective-permute-start = (bf16[1458,288]{0,1:T(8,128)(2,1)}, bf16[1458,288]{0,1:T(8,128)(2,1)S(1)}, u32[]{:S(2)}, u32[]{:S(2)}) collective-permute-start(bf16[1458,288]{0,1:T(8,128)(2,1)} %get-tuple-element.361), channel_id=1, source_target_pairs={{0,4},{4,0},{8,12},{12,8},{1,5},{5,1},{9,13},{13,9},{2,6},{6,2},{1... | collective-permute-start | bytes 2519432 | tf_op jit(solution)/shard_map/ppermute | solution.py:79
  100.0 73.0 %collective-permute-start.1 = (bf16[1458,288]{0,1:T(8,128)(2,1)}, bf16[1458,288]{0,1:T(8,128)(2,1)S(1)}, u32[]{:S(2)}, u32[]{:S(2)}) collective-permute-start(bf16[1458,288]{0,1:T(8,128)(2,1)} %get-tuple-element.363), channel_id=1, source_target_pairs={{0,8},{4,12},{8,0},{12,4},{1,9},{5,13},{9,1},{13,5},{2,10},{6,14},... | collective-permute-start | bytes 2519432 | tf_op jit(solution)/shard_map/ppermute | solution.py:79
  101.6 71.5 %collective-permute-start.2 = (bf16[1458,288]{0,1:T(8,128)(2,1)S(1)}, bf16[1458,288]{0,1:T(8,128)(2,1)S(1)}, u32[]{:S(2)}, u32[]{:S(2)}) collective-permute-start(bf16[1458,288]{0,1:T(8,128)(2,1)S(1)} %get-tuple-element.362), channel_id=1, source_target_pairs={{0,12},{4,8},{8,4},{12,0},{1,13},{5,9},{9,5},{13,1},{2,14},{6,10},... | collective-permute-start | bytes 2519432 | tf_op jit(solution)/shard_map/ppermute | solution.py:79
  171.2 67.4 %collective-permute-start.6 = (bf16[1458,288]{0,1:T(8,128)(2,1)}, bf16[1458,288]{0,1:T(8,128)(2,1)}, u32[]{:S(2)}, u32[]{:S(2)}) collective-permute-start(bf16[1458,288]{0,1:T(8,128)(2,1)} %get-tuple-element.365), channel_id=1, source_target_pairs={{0,4},{4,0},{8,12},{12,8},{1,5},{5,1},{9,13},{13,9},{2,6},{6,2},{1... | collective-permute-start | bytes 2519432 | tf_op jit(solution)/shard_map/ppermute | solution.py:79
  171.2 67.5 %collective-permute-start.7 = (bf16[1458,288]{0,1:T(8,128)(2,1)}, bf16[1458,288]{0,1:T(8,128)(2,1)}, u32[]{:S(2)}, u32[]{:S(2)}) collective-permute-start(bf16[1458,288]{0,1:T(8,128)(2,1)} %get-tuple-element.367), channel_id=1, source_target_pairs={{0,8},{4,12},{8,0},{12,4},{1,9},{5,13},{9,1},{13,5},{2,10},{6,14},... | collective-permute-start | bytes 2519432 | tf_op jit(solution)/shard_map/ppermute | solution.py:79
  172.6 66.0 %collective-permute-start.8 = (bf16[1458,288]{0,1:T(8,128)(2,1)}, bf16[1458,288]{0,1:T(8,128)(2,1)}, u32[]{:S(2)}, u32[]{:S(2)}) collective-permute-start(bf16[1458,288]{0,1:T(8,128)(2,1)} %get-tuple-element.366), channel_id=1, source_target_pairs={{0,12},{4,8},{8,4},{12,0},{1,13},{5,9},{9,5},{13,1},{2,14},{6,10},... | collective-permute-start | bytes 2519432 | tf_op jit(solution)/shard_map/ppermute | solution.py:79
  238.5 77.3 %all-gather.64.cloned.1.call-start = ((), (), s32[]{:S(2)}) async-start(), calls=%async_computation.19 | async-start | bytes 4423680 | tf_op jit(solution)/shard_map/all_gather | solution.py:94
  284.5 146.1 %all-to-all-start = ((bf16[4,1458,288]{1,2,0:T(8,128)(2,1)}), bf16[4,1458,288]{1,2,0:T(8,128)(2,1)}, u32[]{:S(2)}, u32[]{:S(2)}) async-start(bf16[4,1458,288]{1,2,0:T(8,128)(2,1)} %all-gather.54.cloned.1.call-done), calls=%async_computation | async-start | bytes 7077888 | tf_op jit(solution)/shard_map/all_to_all | solution.py:95
  289.4 337.2 %all-gather.48.cloned.1.call-start = ((), (), s32[]{:S(2)}) async-start(), calls=%async_computation.11 | async-start | bytes 11197440 | tf_op jit(solution)/shard_map/all_gather | solution.py:70
  430.7 174.1 %all-to-all-start.2 = ((bf16[4,1458,288]{1,2,0:T(8,128)(2,1)}), bf16[4,1458,288]{1,2,0:T(8,128)(2,1)}, u32[]{:S(2)}, u32[]{:S(2)}) async-start(bf16[4,1458,288]{1,2,0:T(8,128)(2,1)} %all-gather.64.cloned.1.call-done), calls=%async_computation.2 | async-start | bytes 7077888 | tf_op jit(solution)/shard_map/all_to_all | solution.py:95
  435.4 327.3 %all-gather.50.cloned.1.call-start = ((), (), s32[]{:S(2)}) async-start(), calls=%async_computation.12 | async-start | bytes 11197440 | tf_op jit(solution)/shard_map/all_gather | solution.py:70
  440.0 422.0 %all-gather.56.cloned.1.call-start = ((), (), s32[]{:S(2)}) async-start(), calls=%async_computation.15 | async-start | bytes 4423680 | tf_op jit(solution)/shard_map/all_gather | solution.py:70
  625.2 243.5 %all-gather.46.cloned.1.call-start = ((), (), s32[]{:S(2)}) async-start(), calls=%async_computation.10 | async-start | bytes 3317760 | tf_op jit(solution)/shard_map/all_gather | solution.py:87
  625.9 300.1 %all-gather.44.cloned.1.call-start = ((), (), s32[]{:S(2)}) async-start(), calls=%async_computation.9 | async-start | bytes 3317760 | tf_op jit(solution)/shard_map/all_gather | solution.py:89
  626.5 359.7 %all-gather.66.cloned.1.call-start = ((), (), s32[]{:S(2)}) async-start(), calls=%async_computation.20 | async-start | bytes 4423680 | tf_op jit(solution)/shard_map/all_gather | solution.py:70
  790.2 313.2 %all-gather.70.cloned.1.call-start = ((), (), s32[]{:S(2)}) async-start(), calls=%async_computation.22 | async-start | bytes 16588800 | tf_op jit(solution)/shard_map/all_gather | solution.py:94
  811.4 47.4 %collective-permute-start.14 = (bf16[1458,288]{0,1:T(8,128)(2,1)S(1)}, bf16[1458,288]{0,1:T(8,128)(2,1)S(1)}, u32[]{:S(2)}, u32[]{:S(2)}) collective-permute-start(bf16[1458,288]{0,1:T(8,128)(2,1)S(1)} %bitcast.598), channel_id=1, source_target_pairs={{0,12},{4,8},{8,4},{12,0},{1,13},{5,9},{9,5},{13,1},{2,14},{6,10},... | collective-permute-start | bytes 2519432 | tf_op jit(solution)/shard_map/ppermute | solution.py:79
  866.1 36.7 %collective-permute-start.4 = (bf16[1458,288]{0,1:T(8,128)(2,1)}, bf16[1458,288]{0,1:T(8,128)(2,1)}, u32[]{:S(2)}, u32[]{:S(2)}) collective-permute-start(bf16[1458,288]{0,1:T(8,128)(2,1)} %get-tuple-element.355), channel_id=1, source_target_pairs={{0,8},{4,12},{8,0},{12,4},{1,9},{5,13},{9,1},{13,5},{2,10},{6,14},... | collective-permute-start | bytes 2519432 | tf_op jit(solution)/shard_map/ppermute | solution.py:79
  868.7 52.7 %collective-permute-start.5 = (bf16[1458,288]{0,1:T(8,128)(2,1)}, bf16[1458,288]{0,1:T(8,128)(2,1)}, u32[]{:S(2)}, u32[]{:S(2)}) collective-permute-start(bf16[1458,288]{0,1:T(8,128)(2,1)} %get-tuple-element.354), channel_id=1, source_target_pairs={{0,12},{4,8},{8,4},{12,0},{1,13},{5,9},{9,5},{13,1},{2,14},{6,10},... | collective-permute-start | bytes 2519432 | tf_op jit(solution)/shard_map/ppermute | solution.py:79
  940.4 247.9 %all-gather.80.cloned.1.call-start = ((), (), s32[]{:S(2)}) async-start(), calls=%async_computation.27 | async-start | bytes 16588800 | tf_op jit(solution)/shard_map/all_gather | solution.py:94
  945.1 38.0 %collective-permute-start.20 = (bf16[1458,288]{0,1:T(8,128)(2,1)S(1)}, bf16[1458,288]{0,1:T(8,128)(2,1)S(1)}, u32[]{:S(2)}, u32[]{:S(2)}) collective-permute-start(bf16[1458,288]{0,1:T(8,128)(2,1)S(1)} %bitcast.599), channel_id=1, source_target_pairs={{0,12},{4,8},{8,4},{12,0},{1,13},{5,9},{9,5},{13,1},{2,14},{6,10},... | collective-permute-start | bytes 2519432 | tf_op jit(solution)/shard_map/ppermute | solution.py:79
  989.8 41.0 %collective-permute-start.10 = (bf16[1458,288]{0,1:T(8,128)(2,1)S(1)}, bf16[1458,288]{0,1:T(8,128)(2,1)S(1)}, u32[]{:S(2)}, u32[]{:S(2)}) collective-permute-start(bf16[1458,288]{0,1:T(8,128)(2,1)S(1)} %get-tuple-element.359), channel_id=1, source_target_pairs={{0,8},{4,12},{8,0},{12,4},{1,9},{5,13},{9,1},{13,5},{2,10},{6,14},... | collective-permute-start | bytes 2519432 | tf_op jit(solution)/shard_map/ppermute | solution.py:79
  991.6 76.5 %collective-permute-start.11 = (bf16[1458,288]{0,1:T(8,128)(2,1)S(1)}, bf16[1458,288]{0,1:T(8,128)(2,1)S(1)}, u32[]{:S(2)}, u32[]{:S(2)}) collective-permute-start(bf16[1458,288]{0,1:T(8,128)(2,1)S(1)} %get-tuple-element.358), channel_id=1, source_target_pairs={{0,12},{4,8},{8,4},{12,0},{1,13},{5,9},{9,5},{13,1},{2,14},{6,10},... | collective-permute-start | bytes 2519432 | tf_op jit(solution)/shard_map/ppermute | solution.py:79
  1103.5 294.8 %all-to-all-start.4 = ((bf16[4,1458,1076]{1,2,0:T(8,128)(2,1)}), bf16[4,1458,1076]{1,2,0:T(8,128)(2,1)}, u32[]{:S(2)}, u32[]{:S(2)}) async-start(bf16[4,1458,1076]{1,2,0:T(8,128)(2,1)} %all-gather.70.cloned.1.call-done), calls=%async_computation.4 | async-start | bytes 26542080 | tf_op jit(solution)/shard_map/all_to_all | solution.py:95
  1398.3 336.7 %all-to-all-start.6 = ((bf16[4,1458,1076]{1,2,0:T(8,128)(2,1)}), bf16[4,1458,1076]{1,2,0:T(8,128)(2,1)}, u32[]{:S(2)}, u32[]{:S(2)}) async-start(bf16[4,1458,1076]{1,2,0:T(8,128)(2,1)} %all-gather.80.cloned.1.call-done), calls=%async_computation.6 | async-start | bytes 26542080 | tf_op jit(solution)/shard_map/all_to_all | solution.py:95
  1404.7 139.6 %all-gather.72.cloned.1.call-start = ((), (), s32[]{:S(2)}) async-start(), calls=%async_computation.23 | async-start | bytes 3317760 | tf_op jit(solution)/shard_map/all_gather | solution.py:97
  1405.3 384.8 %all-gather.58.cloned.1.call-start = ((), (), s32[]{:S(2)}) async-start(), calls=%async_computation.16 | async-start | bytes 16588800 | tf_op jit(solution)/shard_map/all_gather | solution.py:94
  1405.9 550.9 %all-gather.74.cloned.1.call-start = ((), (), s32[]{:S(2)}) async-start(), calls=%async_computation.24 | async-start | bytes 4423680 | tf_op jit(solution)/shard_map/all_gather | solution.py:70
  1789.5 344.1 %all-gather.68.cloned.1.call-start = ((), (), s32[]{:S(2)}) async-start(), calls=%async_computation.21 | async-start | bytes 16588800 | tf_op jit(solution)/shard_map/all_gather | solution.py:94
  1790.1 408.6 %all-to-all-start.1 = ((bf16[4,1458,1076]{1,2,0:T(8,128)(2,1)}), bf16[4,1458,1076]{1,2,0:T(8,128)(2,1)}, u32[]{:S(2)}, u32[]{:S(2)}) async-start(bf16[4,1458,1076]{1,2,0:T(8,128)(2,1)} %all-gather.58.cloned.1.call-done), calls=%async_computation.1 | async-start | bytes 26542080 | tf_op jit(solution)/shard_map/all_to_all | solution.py:95
  1796.5 410.1 %all-gather.82.cloned.1.call-start = ((), (), s32[]{:S(2)}) async-start(), calls=%async_computation.28 | async-start | bytes 4423680 | tf_op jit(solution)/shard_map/all_gather | solution.py:70
  1960.6 85.0 %collective-permute-start.15 = (bf16[1458,288]{0,1:T(8,128)(2,1)}, bf16[1458,288]{0,1:T(8,128)(2,1)S(1)}, u32[]{:S(2)}, u32[]{:S(2)}) collective-permute-start(bf16[1458,288]{0,1:T(8,128)(2,1)} %get-tuple-element.337), channel_id=1, source_target_pairs={{0,4},{4,0},{8,12},{12,8},{1,5},{5,1},{9,13},{13,9},{2,6},{6,2},{1... | collective-permute-start | bytes 2519432 | tf_op jit(solution)/shard_map/ppermute | solution.py:79
  1960.6 85.0 %collective-permute-start.16 = (bf16[1458,288]{0,1:T(8,128)(2,1)}, bf16[1458,288]{0,1:T(8,128)(2,1)S(1)}, u32[]{:S(2)}, u32[]{:S(2)}) collective-permute-start(bf16[1458,288]{0,1:T(8,128)(2,1)} %get-tuple-element.339), channel_id=1, source_target_pairs={{0,8},{4,12},{8,0},{12,4},{1,9},{5,13},{9,1},{13,5},{2,10},{6,14},... | collective-permute-start | bytes 2519432 | tf_op jit(solution)/shard_map/ppermute | solution.py:79
  1962.0 83.6 %collective-permute-start.17 = (bf16[1458,288]{0,1:T(8,128)(2,1)}, bf16[1458,288]{0,1:T(8,128)(2,1)S(1)}, u32[]{:S(2)}, u32[]{:S(2)}) collective-permute-start(bf16[1458,288]{0,1:T(8,128)(2,1)} %get-tuple-element.338), channel_id=1, source_target_pairs={{0,12},{4,8},{8,4},{12,0},{1,13},{5,9},{9,5},{13,1},{2,14},{6,10},... | collective-permute-start | bytes 2519432 | tf_op jit(solution)/shard_map/ppermute | solution.py:79
  2045.5 524.2 %all-gather.76.cloned.1.call-start = ((), (), s32[]{:S(2)}) async-start(), calls=%async_computation.25 | async-start | bytes 13117440 | tf_op jit(solution)/shard_map/all_gather | solution.py:94
  2198.7 371.0 %all-to-all-start.3 = ((bf16[4,1458,1076]{1,2,0:T(8,128)(2,1)}), bf16[4,1458,1076]{1,2,0:T(8,128)(2,1)}, u32[]{:S(2)}, u32[]{:S(2)}) async-start(bf16[4,1458,1076]{1,2,0:T(8,128)(2,1)} %all-gather.68.cloned.1.call-done), calls=%async_computation.3 | async-start | bytes 26542080 | tf_op jit(solution)/shard_map/all_to_all | solution.py:95
  2205.1 370.9 %all-gather.78.cloned.1.call-start = ((), (), s32[]{:S(2)}) async-start(), calls=%async_computation.26 | async-start | bytes 2580480 | tf_op jit(solution)/shard_map/all_gather | solution.py:97
  2206.5 375.0 %all-gather.60.cloned.1.call-start = ((), (), s32[]{:S(2)}) async-start(), calls=%async_computation.17 | async-start | bytes 3317760 | tf_op jit(solution)/shard_map/all_gather | solution.py:99
  2210.2 41.7 %collective-permute-start.22 = (bf16[1458,288]{0,1:T(8,128)(2,1)}, bf16[1458,288]{0,1:T(8,128)(2,1)S(1)}, u32[]{:S(2)}, u32[]{:S(2)}) collective-permute-start(bf16[1458,288]{0,1:T(8,128)(2,1)} %get-tuple-element.343), channel_id=1, source_target_pairs={{0,8},{4,12},{8,0},{12,4},{1,9},{5,13},{9,1},{13,5},{2,10},{6,14},... | collective-permute-start | bytes 2519432 | tf_op jit(solution)/shard_map/ppermute | solution.py:79
  2211.1 73.5 %collective-permute-start.23 = (bf16[1458,288]{0,1:T(8,128)(2,1)S(1)}, bf16[1458,288]{0,1:T(8,128)(2,1)S(1)}, u32[]{:S(2)}, u32[]{:S(2)}) collective-permute-start(bf16[1458,288]{0,1:T(8,128)(2,1)S(1)} %get-tuple-element.342), channel_id=1, source_target_pairs={{0,12},{4,8},{8,4},{12,0},{1,13},{5,9},{9,5},{13,1},{2,14},{6,10},... | collective-permute-start | bytes 2519432 | tf_op jit(solution)/shard_map/ppermute | solution.py:79
  2212.0 730.2 %all-gather.84.cloned.1.call-start = ((), (), s32[]{:S(2)}) async-start(), calls=%async_computation.29 | async-start | bytes 13117440 | tf_op jit(solution)/shard_map/all_gather | solution.py:94
  2569.7 372.5 %all-to-all-start.5 = ((bf16[4,1458,864]{2,1,0:T(8,128)(2,1)}), bf16[4,1458,864]{2,1,0:T(8,128)(2,1)}, u32[]{:S(2)}, u32[]{:S(2)}) async-start(bf16[4,1458,864]{2,1,0:T(8,128)(2,1)} %all-gather.76.cloned.1.call-done), calls=%async_computation.5 | async-start | bytes 20987904 | tf_op jit(solution)/shard_map/all_to_all | solution.py:95
  2942.2 311.8 %all-to-all-start.7 = ((bf16[4,1458,864]{2,1,0:T(8,128)(2,1)}), bf16[4,1458,864]{2,1,0:T(8,128)(2,1)}, u32[]{:S(2)}, u32[]{:S(2)}) async-start(bf16[4,1458,864]{2,1,0:T(8,128)(2,1)} %all-gather.84.cloned.1.call-done), calls=%async_computation.7 | async-start | bytes 20987904 | tf_op jit(solution)/shard_map/all_to_all | solution.py:95
  2948.2 288.2 %all-reduce.9.cloned.1.call-start = ((), (), s32[]{:S(2)}) async-start(), calls=%async_computation.30 | async-start | bytes 8847360 | tf_op jit(solution)/shard_map/psum | solution.py:148
  (139 other events, 4489.2 us)
Sparse Core Ops, SparseCore 0:
  26.2 70.3 all-gather.51
  98.6 68.5 all-gather.61
  168.8 32.1 all-gather.41
  238.7 30.7 all-gather.53
  284.6 31.2 all-gather.63
  317.3 286.3 all-gather.47
  605.3 157.4 all-gather.49
  764.9 68.1 all-gather.55
  834.7 31.8 all-gather.45
  868.0 39.2 all-gather.43
  909.5 69.9 all-gather.65
  980.9 122.5 all-gather.69
  1105.0 83.2 all-gather.79
  1406.8 137.4 all-gather.71
  1545.8 83.2 all-gather.57
  1789.6 167.0 all-gather.73
  1958.2 121.4 all-gather.67
  2081.6 96.6 all-gather.81
  2179.9 102.1 all-gather.75
  2283.5 74.3 all-gather.77
  2359.5 189.4 all-gather.59
  2550.5 68.9 all-gather.83
  3121.6 114.7 all-reduce.8
